TPU v7x, 512 devices: a whole 4x8x8 slice. The times are simulated.
512 devices in a mesh: ctx: 32 (over x, y), pair: 16 (over z, core).
Axes of the slice: x: 4, y: 8, z: 8, core: 2. Of those that a mesh axis runs over, the one named last changes fastest.
Arguments:
- prompt_x: bfloat16 [2, 8192, 16384], P(None, 'ctx', 'pair'), may hold values from -6 to 6
- prompt_bc: bfloat16 [2, 2, 16, 8192], P(None, None, None, 'ctx'), may hold values from -3 to 3
- prompt_logdec: float32 [2, 256, 8192], P(None, 'pair', 'ctx'), may hold values from -2.5 to 0, as said below
- branch_x: bfloat16 [32, 512, 16384], P('pair', None, 'ctx'), may hold values from -6 to 6
- branch_bc: bfloat16 [2, 32, 16, 512], P(None, 'pair'), may hold values from -3 to 3
- branch_logdec: float32 [32, 256, 512], P('pair', 'ctx'), may hold values from -2.5 to 0, as said below
- branch_prompt: int32 [16], P('pair'), may hold values from 0 to 1
- branch_len: int32 [32], P('pair'), may hold values from 128 to 512, as said below
Outputs:
- prompt_y: bfloat16 [2, 8192, 16384], P(None, 'ctx', 'pair')
- branch_y: bfloat16 [32, 512, 16384], P('pair', None, 'ctx')
Inputs may be any that keep to these rules, and one draw needn't show every extreme that they name: `prompt_logdec`: the logarithm of a position's decay for each head. `branch_logdec`: the logarithm of a position's decay for each head. `branch_len`: positions of a branch at or after its length are masked; some branch has all 512 positions live.
All inputs are finite; a program needn't handle non-finite values.
Results may differ from a plain program's by a relative error of at most 0.0049.
Values sent between devices are 32-bit elements; how exact they have to be, the bound alone decides.
A program may use at most 64 MiB of HBM per device.

v0:
```python
import jax
import jax.numpy as jnp
from jax import lax
from jax.sharding import Mesh
from jax.sharding import PartitionSpec as P

BLOCK = 256
CTX = ("ctx_0", "ctx_1")


def nothing_yet(array, identity):
    return jax.tree.map(
        lambda a, e: jnp.broadcast_to(jnp.asarray(e, a.dtype), a.shape), array, identity
    )


def carried_in(array, axes, combine, identity):
    before = start = nothing_yet(array, identity)
    total = array
    for axis in reversed(axes):
        size, mine = (lax.axis_size(axis), lax.axis_index(axis))
        pieces = jax.tree.map(lambda part: lax.all_gather(part, axis), total)
        inside, total = (start, start)
        for k in range(size):
            passed = k < mine
            total = combine(total, jax.tree.map(lambda part: part[k], pieces))
            inside = jax.tree.map(lambda new, old: jnp.where(passed, new, old), total, inside)
        before = combine(inside, before)
    return before


def laid_out(pieces, dim):
    dims = list(pieces.shape[1:])
    dims[dim] *= pieces.shape[0]
    return jnp.moveaxis(pieces, 0, dim).reshape(dims)


def copy_for_each(array, axis):
    size = lax.axis_size(axis)
    return lax.all_to_all(
        jnp.broadcast_to(array[None], (size, *array.shape)), axis, 0, 0, tiled=True
    )


def collect(array, axis, dim):
    return laid_out(copy_for_each(array, axis), dim)


def cut_along(array, dim, size):
    dims = array.shape
    pieces = array.reshape(*dims[:dim], size, dims[dim] // size, *dims[dim + 1 :])
    return jnp.moveaxis(pieces, dim, 0)


def sent_and_summed(array, axis, dim):
    pieces = cut_along(array, dim, lax.axis_size(axis))
    arrived = lax.all_to_all(pieces, axis, split_axis=0, concat_axis=0, tiled=True)
    return arrived.sum(axis=0)


def rows_for(lines, size):
    spare = -lines.shape[0] % size
    if not spare:
        return lines
    return jnp.concatenate([lines, jnp.zeros((spare, *lines.shape[1:]), lines.dtype)])


def total_of(array, axes):
    lines = array.reshape(-1, array.shape[-1])
    own = sent_and_summed(rows_for(lines, lax.axis_size(axes)), axes, 0)
    whole = collect(own, axes, 0)
    return whole[: len(lines)].reshape(array.shape)


def broadcast(array, axis, root):
    return lax.dynamic_index_in_dim(lax.all_gather(array, axis), root, 0, keepdims=False)


def block_pass(inputs, log_decay, b_rows, c_rows, start_state):
    block_rows, channels = inputs.shape
    head_count = log_decay.shape[0]
    head_width = channels // head_count
    running = jnp.cumsum(log_decay, axis=1)
    in_gain = jnp.sqrt(-jnp.expm1(2.0 * log_decay))
    scores = jnp.dot(c_rows.T, b_rows, preferred_element_type=jnp.float32)
    row_ids = lax.broadcasted_iota(jnp.int32, (block_rows, block_rows), 0)
    col_ids = lax.broadcasted_iota(jnp.int32, (block_rows, block_rows), 1)
    causal = (col_ids <= row_ids)[None, :, :]
    to_end = jnp.exp(running[:, -1:] - running) * in_gain
    inject = (b_rows.astype(jnp.float32)[None, :, :] * to_end[:, None, :]).astype(jnp.bfloat16)
    by_head = inputs.reshape(block_rows, head_count, head_width)
    differ = jnp.where(causal, running[:, :, None] - running[:, None, :], 0.0)
    weights = jnp.where(causal, jnp.exp(differ), 0.0)
    weights = (scores[None, :, :] * weights * in_gain[:, None, :]).astype(jnp.bfloat16)
    inner_out = jnp.einsum(
        "hts,shp->thp", weights, by_head, preferred_element_type=jnp.float32
    ).reshape(block_rows, channels)
    states = jnp.einsum("hns,shp->hnp", inject, by_head, preferred_element_type=jnp.float32)
    projected = jnp.einsum(
        "nt,hnp->thp", c_rows.astype(jnp.float32), start_state, precision=lax.Precision.HIGHEST
    )
    carried = (projected * jnp.exp(running).T[:, :, None]).reshape(block_rows, channels)
    end_state = jnp.exp(running[:, -1])[:, None, None] * start_state + states
    return (inner_out + carried, end_state)


def run_blocks(inputs, log_decay, b_and_c, start_state):
    sequence_length, channels = inputs.shape
    head_count = log_decay.shape[0]
    state_size = b_and_c.shape[1]
    block_count = sequence_length // BLOCK
    input_blocks = inputs.reshape(block_count, BLOCK, channels)
    decay_blocks = jnp.transpose(log_decay.reshape(head_count, block_count, BLOCK), (1, 0, 2))
    proj_blocks = jnp.transpose(b_and_c.reshape(2, state_size, block_count, BLOCK), (2, 0, 1, 3))

    def advance(carry_state, pieces):
        block_in, block_decay, block_proj = pieces
        block_out, end_state = block_pass(
            block_in, block_decay, block_proj[0], block_proj[1], carry_state
        )
        return (end_state, block_out)

    end_state, outputs = lax.scan(advance, start_state, (input_blocks, decay_blocks, proj_blocks))
    return (outputs.reshape(sequence_length, channels), end_state)


def carried_term(c_rows, log_decay, start_state):
    running = jnp.cumsum(log_decay, axis=1)
    projected = jnp.einsum(
        "nt,hnp->thp", c_rows.astype(jnp.float32), start_state, precision=lax.Precision.HIGHEST
    )
    return (projected * jnp.exp(running).T[:, :, None]).reshape(c_rows.shape[1], -1)


def chain_step(earlier, later):
    return (earlier[0] + later[0], jnp.exp(later[0])[:, :, None, None] * earlier[1] + later[1])


def body(
    prompt_x,
    prompt_bc,
    prompt_logdec,
    branch_x,
    branch_bc,
    branch_logdec,
    branch_prompt,
    branch_len,
):
    prompts = prompt_x.shape[0]
    branches = branch_x.shape[0]
    heads_here = prompt_logdec.shape[1]
    branch_heads = branch_logdec.shape[1]
    state_size = prompt_bc.shape[2]
    head_width = prompt_x.shape[2] // heads_here
    zero_state = jnp.zeros((heads_here, state_size, head_width), jnp.float32)
    local_outs = []
    local_ends = []
    for prompt_id in range(prompts):
        result, end_state = run_blocks(
            prompt_x[prompt_id], prompt_logdec[prompt_id], prompt_bc[:, prompt_id], zero_state
        )
        local_outs.append(result)
        local_ends.append(end_state)
    local_ends = jnp.stack(local_ends)
    totals = jnp.sum(prompt_logdec, axis=2)
    identity = (jnp.zeros_like(totals), jnp.zeros_like(local_ends))
    before_log, before = carried_in((totals, local_ends), CTX, chain_step, identity)
    prompt_y = jnp.stack(
        [
            (
                local_outs[prompt_id]
                + carried_term(prompt_bc[1, prompt_id], prompt_logdec[prompt_id], before[prompt_id])
            ).astype(jnp.bfloat16)
            for prompt_id in range(prompts)
        ]
    )
    ctx_pos = lax.axis_index(CTX)
    everyone = collect(totals[None], CTX, 0)
    later_parts = (jnp.arange(lax.axis_size(CTX), dtype=jnp.int32) > ctx_pos).astype(jnp.float32)
    suffix = jnp.sum(everyone * later_parts[:, None, None], axis=0)
    final_state = total_of(jnp.exp(suffix)[:, :, None, None] * local_ends, CTX)
    owner_id = ctx_pos * branch_heads // heads_here
    offset = ctx_pos * branch_heads - owner_id * heads_here
    my_piece = lax.dynamic_slice_in_dim(final_state, offset, branch_heads, 1)
    my_states = broadcast(my_piece, "pair", owner_id)
    token_positions = lax.broadcasted_iota(jnp.int32, (branch_x.shape[1], 1), 0)
    outputs = []
    for branch_id in range(branches):
        source = branch_prompt[branch_id // 2]
        picked = source == jnp.arange(prompts, dtype=jnp.int32)
        start_state = jnp.sum(jnp.where(picked[:, None, None, None], my_states, 0.0), axis=0)
        branch_out, unused_end = run_blocks(
            branch_x[branch_id], branch_logdec[branch_id], branch_bc[:, branch_id], start_state
        )
        outputs.append(
            jnp.where(token_positions < branch_len[branch_id], branch_out, 0.0).astype(jnp.bfloat16)
        )
    return (prompt_y, jnp.stack(outputs))


def solution(mesh):
    finer = Mesh(mesh.devices.reshape(4, 8, mesh.shape["pair"]), ("ctx_0", "ctx_1", "pair"))
    return jax.shard_map(
        body,
        mesh=finer,
        in_specs=(
            P(None, CTX, "pair"),
            P(None, None, None, CTX),
            P(None, "pair", CTX),
            P("pair", None, CTX),
            P(None, "pair", None, None),
            P("pair", CTX, None),
            P("pair"),
            P("pair"),
        ),
        out_specs=(P(None, CTX, "pair"), P("pair", None, CTX)),
        check_vma=False,
    )
```

profile of v0, /device:TPU:7, one launch (start us, length us, event | category | flops | bytes accessed | tf_op | source)
XLA Modules:
  0.0 163.7 jit_solution(14940731348543095993)
XLA Ops:
  7.2 1.4 sqrt_bitcast_fusion.3
  8.6 0.6 reduce-window.38
  9.4 0.6 reduce-window.36
  10.7 1.3 exponential_multiply_fusion.3
  12.0 1.3 fusion.122
  14.3 0.7 pad_maximum_fusion.2
  15.2 0.6 broadcast_in_dim.215
  15.8 9.7 %all-to-all-start = ((f32[32,1,2,16]{3,2,1,0:T(2,128)}), f32[32,1,2,16]{3,2,1,0:T(2,128)S(1)}, u32[]{:S(2)}, u32[]{:S(2)}) async-start(f32[32,1,2,16]{3,2,1,0:T(2,128)} %broadcast_in_dim.215), calls=%async_computation | async-start | bytes 65536 | tf_op jit(solution)/shard_map/all_to_all | solution.py:40
  25.8 13.8 %all-gather.3 = f32[8,2,16]{2,1,0:T(2,128)S(1)} all-gather(f32[1,2,16]{2,1,0:T(2,128)S(1)} %bitcast.420), channel_id=2, replica_groups=mesh['ctx_0'=4,'ctx_1'=8,'pair'=16] {'ctx_1'}, dimensions={0}, use_global_device_ids=true | all-gather | bytes 1152 | tf_op jit(solution)/shard_map/all_gather | solution.py:22
  39.6 0.6 fusion.116
  40.2 0.6 bitcast_add_fusion.8
  40.8 0.6 fusion.115
  41.4 5.4 %all_gather.28 = f32[4,2,16]{2,1,0:T(2,128)S(1)} all-gather(f32[1,2,16]{2,1,0:T(2,128)S(1)} %get-tuple-element.197), channel_id=1, replica_groups=mesh['ctx_0'=4,'ctx_1'=8,'pair'=16] {'ctx_0'}, dimensions={0}, use_global_device_ids=true | all-gather | bytes 640 | tf_op jit(solution)/shard_map/all_gather | solution.py:22
  46.8 0.6 fusion.110
  47.4 0.6 fusion.125
  48.0 1.2 iota_compare_fusion.3
  49.8 0.6 fusion.124
  50.5 1.4 fusion.50
  51.9 0.5 fusion.55
  52.4 0.5 iota_compare_fusion.5
  53.3 0.8 reshape.905
  54.1 7.2 %all-to-all-start.1 = ((f32[32,1,1024]{2,1,0:T(1,128)}), f32[32,1,1024]{2,1,0:T(1,128)S(1)}, u32[]{:S(2)}, u32[]{:S(2)}) async-start(f32[32,1,1024]{2,1,0:T(1,128)} %reshape.905), calls=%async_computation.1 | async-start | bytes 262144 | tf_op jit(solution)/shard_map/all_to_all | solution.py:57
  61.3 1.1 iota_compare_fusion.4
  62.5 0.6 copy.98
  63.1 0.6 copy.95
  63.9 4.9 %all-to-all-done.1 = f32[32,1,1024]{2,1,0:T(1,128)S(1)} async-done(((f32[32,1,1024]{2,1,0:T(1,128)}), f32[32,1,1024]{2,1,0:T(1,128)S(1)}, u32[]{:S(2)}, u32[]{:S(2)}) %all-to-all-start.1) | async-done | bytes 131104 | tf_op jit(solution)/shard_map/all_to_all | solution.py:57
  68.9 0.5 broadcast.347
  69.4 0.9 reduce.16
  70.5 0.8 reshape.907
  71.4 5.5 %all-to-all-start.2 = ((f32[32,1,1024]{2,1,0:T(1,128)}), f32[32,1,1024]{2,1,0:T(1,128)S(1)}, u32[]{:S(2)}, u32[]{:S(2)}) async-start(f32[32,1,1024]{2,1,0:T(1,128)} %reshape.907), calls=%async_computation.2 | async-start | bytes 262144 | tf_op jit(solution)/shard_map/all_to_all | solution.py:40
  76.9 1.3 fusion.121
  78.2 6.2 %all-to-all-done.2 = f32[32,1,1024]{2,1,0:T(1,128)S(1)} async-done(((f32[32,1,1024]{2,1,0:T(1,128)}), f32[32,1,1024]{2,1,0:T(1,128)S(1)}, u32[]{:S(2)}, u32[]{:S(2)}) %all-to-all-start.2) | async-done | bytes 131104 | tf_op jit(solution)/shard_map/all_to_all | solution.py:40
  84.3 0.9 reduce.17
  85.3 0.7 constant_dynamic-slice_fusion.2
  86.1 1.4 fusion.51
  87.6 0.5 fusion.59
  88.3 2.0 %bitcast_add_fusion = f32[1,2,16,16,64]{4,3,2,1,0:T(8,128)S(1)} fusion(f32[16,16,16,64]{3,2,1,0:T(8,128)} %all-gather.7.cloned.1.call-done, f32[2,16]{1,0:T(2,128)S(1)} %copy-done.20, f32[2,16]{1,0:T(2,128)S(1)} %copy-done.19, f32[2,16]{1,0:T(2,128)S(1)} %copy-done.23, f32[2,16]{1,0:T(2,128)S(1)} %copy-done.21, f32[2,16]{1,0:T(2,128)S(1)} %copy-done.22, ...), kind=kLoop, calls=%fused_computation.123 | loop fusion | flops 491520 | bytes 1180672 | tf_op jit(solution)/shard_map/add | solution.py:136
  90.3 11.1 %all_gather.31 = f32[4,2,16,16,64]{4,3,2,1,0:T(8,128)S(1)} all-gather(f32[1,2,16,16,64]{4,3,2,1,0:T(8,128)S(1)} %bitcast_add_fusion), channel_id=1, replica_groups=mesh['ctx_0'=4,'ctx_1'=8,'pair'=16] {'ctx_0'}, dimensions={0}, use_global_device_ids=true | all-gather | bytes 655360 | tf_op jit(solution)/shard_map/all_gather | solution.py:22
  101.4 0.5 fusion.69
  102.0 1.4 fusion.61
  103.4 1.2 copy.93
  104.7 0.6 fusion.60
  105.5 1.1 pad_maximum_fusion
  106.6 30.5 %all-gather.9.cloned.1.call-done = f32[32,8,16,64]{3,2,1,0:T(8,128)} async-done(((f32[2,8,16,64]{3,2,1,0:T(8,128)}), f32[32,8,16,64]{3,2,1,0:T(8,128)}) %all-gather.9.cloned.1.call-update) | async-done | bytes 1048592 | tf_op jit(solution)/shard_map/all_gather | solution.py:76
  137.1 1.0 fusion.80
  138.2 10.7 %while.5 = (s32[]{:T(128)}, f32[8,16,64]{2,1,0:T(8,128)S(1)}, bf16[2,256,512]{2,1,0:T(8,128)(2,1)S(1)}, f32[2,8,256]{2,1,0:T(8,128)S(1)}, bf16[2,2,16,256]{3,2,1...) while((s32[]{:T(128)}, f32[8,16,64]{2,1,0:T(8,128)S(1)}, ...), condition=%wide.region_15.16_spmd, body=%wide.region_12.15_spmd.sunk | while | flops 102527000 | bytes 4876605 | solution.py:123
  138.2 0.6 reduce-window.54
  139.1 1.1 convolution_multiply_fusion.5
  140.6 0.7 fusion.165
  141.5 0.9 fusion.166
  142.5 0.8 fusion.167
  143.5 0.6 reduce-window.54
  144.4 1.1 convolution_multiply_fusion.5
  146.0 0.7 fusion.165
  146.9 0.9 fusion.166
  147.8 0.8 fusion.167
  148.9 6.5 %while.4 = (s32[]{:T(128)}, f32[8,16,64]{2,1,0:T(8,128)S(1)}, bf16[2,256,512]{2,1,0:T(8,128)(2,1)S(1)}, f32[2,8,256]{2,1,0:T(8,128)S(1)}, bf16[2,2,16,256]{3,2,1...) while((s32[]{:T(128)}, f32[8,16,64]{2,1,0:T(8,128)S(1)}, ...), condition=%wide.region_11.12_spmd, body=%wide.region_8.11_spmd.sunk | while | flops 102527000 | bytes 4909373 | solution.py:123
  148.9 0.6 reduce-window.52
  149.8 0.4 convolution_multiply_fusion.4
  151.2 0.8 fusion.159
  152.2 0.6 reduce-window.52
  153.0 0.4 convolution_multiply_fusion.4
  154.4 0.8 fusion.159
  155.8 1.1 pad_maximum_fusion.1
  (178 shorter events, 8.7 us)
Async XLA Ops:
  7.2 6.4 %copy-start.5 = (bf16[2,2,16,256]{3,2,1,0:T(8,128)(2,1)S(1)}, bf16[2,2,16,256]{3,2,1,0:T(8,128)(2,1)}, u32[]{:S(2)}) copy-start(bf16[2,2,16,256]{3,2,1,0:T(8,128)(2,1)} %param.13) | copy-start | bytes 98308
  7.2 81.0 %all-gather.7.cloned.1.call-start = ((), (), s32[]{:S(2)}) async-start(), calls=%async_computation.3 | async-start | bytes 2359296 | tf_op jit(solution)/shard_map/all_gather | solution.py:22
  10.3 3.0 %copy-start.13 = (f32[2,2,8,128]{3,2,0,1:T(8,128)}, f32[2,2,8,128]{3,2,0,1:T(8,128)S(1)}, u32[]{:S(2)}) copy-start(f32[2,2,8,128]{3,2,0,1:T(8,128)S(1)} %copy.129) | copy-start | bytes 49156
  12.0 39.8 %copy-start.8 = (f32[256,16]{0,1:T(8,128)}, f32[256,16]{0,1:T(8,128)S(1)}, u32[]{:S(2)}) copy-start(f32[256,16]{0,1:T(8,128)S(1)} %get-tuple-element.214) | copy-start | bytes 49156
  13.3 1.7 %copy-start.4 = (f32[2,16,256]{2,1,0:T(8,128)S(1)}, f32[2,16,256]{2,1,0:T(8,128)}, u32[]{:S(2)}) copy-start(f32[2,16,256]{2,1,0:T(8,128)} %param.14) | copy-start | bytes 98308
  13.6 33.8 %copy-start.30 = (s32[2]{0:T(128)S(1)}, s32[2]{0:T(128)}, u32[]{:S(2)}) copy-start(s32[2]{0:T(128)} %param.19) | copy-start | bytes 28
  13.6 36.3 %copy-start.15 = (f32[2,8,512]{2,1,0:T(8,128)S(1)}, f32[2,8,512]{2,1,0:T(8,128)}, u32[]{:S(2)}) copy-start(f32[2,8,512]{2,1,0:T(8,128)} %param.17) | copy-start | bytes 98308
  13.6 36.9 %copy-start.10 = (bf16[2,2,16,512]{3,2,1,0:T(8,128)(2,1)S(1)}, bf16[2,2,16,512]{3,2,1,0:T(8,128)(2,1)}, u32[]{:S(2)}) copy-start(bf16[2,2,16,512]{3,2,1,0:T(8,128)(2,1)} %param.16) | copy-start | bytes 196612
  15.8 37.1 %all-to-all-start = ((f32[32,1,2,16]{3,2,1,0:T(2,128)}), f32[32,1,2,16]{3,2,1,0:T(2,128)S(1)}, u32[]{:S(2)}, u32[]{:S(2)}) async-start(f32[32,1,2,16]{3,2,1,0:T(2,128)} %broadcast_in_dim.215), calls=%async_computation | async-start | bytes 65536 | tf_op jit(solution)/shard_map/all_to_all | solution.py:40
  25.7 26.1 %copy-start.11 = (pred[256,256]{1,0:T(8,128)(4,1)}, pred[256,256]{1,0:T(8,128)(4,1)S(1)}, u32[]{:S(2)}) copy-start(pred[256,256]{1,0:T(8,128)(4,1)S(1)} %iota_compare_fusion.2) | copy-start | bytes 196612
  51.8 1.3 copy-start.1
  54.1 14.8 %all-to-all-start.1 = ((f32[32,1,1024]{2,1,0:T(1,128)}), f32[32,1,1024]{2,1,0:T(1,128)S(1)}, u32[]{:S(2)}, u32[]{:S(2)}) async-start(f32[32,1,1024]{2,1,0:T(1,128)} %reshape.905), calls=%async_computation.1 | async-start | bytes 262144 | tf_op jit(solution)/shard_map/all_to_all | solution.py:57
  70.5 15.6 %copy-start.12 = (pred[256,256]{1,0:T(8,128)(4,1)S(1)}, pred[256,256]{1,0:T(8,128)(4,1)}, u32[]{:S(2)}) copy-start(pred[256,256]{1,0:T(8,128)(4,1)} %copy-done.11) | copy-start | bytes 196612
  70.5 15.6 %copy-start.14 = (f32[2,2,8,128]{3,2,0,1:T(8,128)S(1)}, f32[2,2,8,128]{3,2,0,1:T(8,128)}, u32[]{:S(2)}) copy-start(f32[2,2,8,128]{3,2,0,1:T(8,128)} %copy-done.13) | copy-start | bytes 49156
  70.5 15.6 %copy-start.16 = (f32[16,256]{1,0:T(8,128)S(1)}, f32[16,256]{1,0:T(8,128)}, u32[]{:S(2)}) copy-start(f32[16,256]{1,0:T(8,128)} %get-tuple-element.206) | copy-start | bytes 49156
  71.4 13.0 %all-to-all-start.2 = ((f32[32,1,1024]{2,1,0:T(1,128)}), f32[32,1,1024]{2,1,0:T(1,128)S(1)}, u32[]{:S(2)}, u32[]{:S(2)}) async-start(f32[32,1,1024]{2,1,0:T(1,128)} %reshape.907), calls=%async_computation.2 | async-start | bytes 262144 | tf_op jit(solution)/shard_map/all_to_all | solution.py:40
  76.8 60.3 %all-gather.9.cloned.1.call-start = ((), (), s32[]{:S(2)}) async-start(), calls=%async_computation.4 | async-start | bytes 2228224 | tf_op jit(solution)/shard_map/all_gather | solution.py:76
  86.1 1.5 copy-start.6
  86.1 1.5 copy-start.7
  87.5 0.7 copy-start.17
  87.5 0.7 copy-start.18
  87.5 0.7 copy-start.19
  87.5 0.7 copy-start.20
  87.5 0.7 copy-start.21
  87.5 0.7 copy-start.22
  87.5 0.7 copy-start.23
  87.5 0.7 copy-start.24
  88.1 13.3 %copy-start.25 = (f32[2,16]{1,0:T(2,128)S(1)}, f32[2,16]{1,0:T(2,128)}, u32[]{:S(2)}) copy-start(f32[2,16]{1,0:T(2,128)} %get-tuple-element.196) | copy-start | bytes 388
  88.1 13.3 %copy-start.26 = (f32[2,16]{1,0:T(2,128)S(1)}, f32[2,16]{1,0:T(2,128)}, u32[]{:S(2)}) copy-start(f32[2,16]{1,0:T(2,128)} %get-tuple-element.224) | copy-start | bytes 388
  88.1 13.3 %copy-start.27 = (f32[2,16]{1,0:T(2,128)S(1)}, f32[2,16]{1,0:T(2,128)}, u32[]{:S(2)}) copy-start(f32[2,16]{1,0:T(2,128)} %get-tuple-element.225) | copy-start | bytes 388
  88.1 13.3 %copy-start.28 = (f32[2,16]{1,0:T(2,128)S(1)}, f32[2,16]{1,0:T(2,128)}, u32[]{:S(2)}) copy-start(f32[2,16]{1,0:T(2,128)} %get-tuple-element.226) | copy-start | bytes 388
  88.1 13.3 %copy-start.29 = (f32[2,16]{1,0:T(2,128)S(1)}, f32[2,16]{1,0:T(2,128)}, u32[]{:S(2)}) copy-start(f32[2,16]{1,0:T(2,128)} %get-tuple-element.227) | copy-start | bytes 388
  88.2 13.2 %copy-start = (f32[16,16,16,64]{3,2,1,0:T(8,128)S(1)}, f32[16,16,16,64]{3,2,1,0:T(8,128)}, u32[]{:S(2)}) copy-start(f32[16,16,16,64]{3,2,1,0:T(8,128)} %all-gather.7.cloned.1.call-done) | copy-start | bytes 3145732
  90.3 11.7 %copy-start.9 = (f32[256,16]{0,1:T(8,128)S(1)}, f32[256,16]{0,1:T(8,128)}, u32[]{:S(2)}) copy-start(f32[256,16]{0,1:T(8,128)} %copy-done.8) | copy-start | bytes 49156
  104.7 32.4 %copy-start.33 = (pred[2]{0:T(512)(128)(4,1)S(1)}, pred[2]{0:T(512)(128)(4,1)}, u32[]{:S(2)}) copy-start(pred[2]{0:T(512)(128)(4,1)} %iota_compare_fusion.5) | copy-start | bytes 10
  105.3 32.9 %copy-start.3 = (f32[1,8,512]{2,1,0:T(8,128)S(1)}, f32[1,8,512]{2,1,0:T(8,128)}, u32[]{:S(2)}) copy-start(f32[1,8,512]{2,1,0:T(8,128)} %get-tuple-element.205) | copy-start | bytes 49156
  138.2 10.7 %copy-start.2 = (bf16[2,2,16,256]{3,2,1,0:T(8,128)(2,1)S(1)}, bf16[2,2,16,256]{3,2,1,0:T(8,128)(2,1)}, u32[]{:S(2)}) copy-start(bf16[2,2,16,256]{3,2,1,0:T(8,128)(2,1)} %copy.95) | copy-start | bytes 98308
  148.9 6.5 %copy-start.31 = (pred[512]{0:T(512)(128)(4,1)S(1)}, pred[512]{0:T(512)(128)(4,1)}, u32[]{:S(2)}) copy-start(pred[512]{0:T(512)(128)(4,1)} %iota_compare_fusion.3) | copy-start | bytes 1540
  148.9 6.7 %copy-start.32 = (pred[512]{0:T(512)(128)(4,1)S(1)}, pred[512]{0:T(512)(128)(4,1)}, u32[]{:S(2)}) copy-start(pred[512]{0:T(512)(128)(4,1)} %iota_compare_fusion.4) | copy-start | bytes 1540
Sparse Core Ops, SparseCore 0:
  15.2 43.4 all-gather.6
  86.1 50.8 all-gather.8
where the time goes:
time: 166 us; the launch traced here: 164 us
  waiting for transfers between devices  41.7 us (25%)
  blocking collectives  30.3 us (18%)
  starting transfers between devices  22.4 us (13%)
  other arithmetic  22.3 us (13%)
  matrix products  16.2 us (10%)
  between operations  15.4 us (9%)
  local copies, waits for them, and re-layouts  14.9 us (9%)
    all_gather x1, waiting for transfers between devices, broadcast(): lax.all_gather(array, axis)  30.5 us
    all_gather x3, blocking collectives, carried_in(): pieces = jax.tree.map(lambda part: lax.all_gather(part, axis), total)  30.3 us
    all_to_all x2, starting transfers between devices, copy_for_each(): lax.all_to_all(jnp.broadcast_to(array[None], (size, *array.shape)), axis,...  15.1 us
    all_to_all x1, starting transfers between devices, sent_and_summed(): lax.all_to_all(pieces, axis, split_axis=0, concat_axis=0, tiled=True)  7.21 us
    all_to_all x2, waiting for transfers between devices, copy_for_each(): lax.all_to_all(jnp.broadcast_to(array[None], (size, *array.shape)), axis,...  6.17 us
    dot_general x6, matrix products, block_pass(): jnp.einsum('hts,shp->thp', weights, by_head, preferred_element_type=jnp.f...  6.01 us
    all_to_all x1, waiting for transfers between devices, sent_and_summed(): lax.all_to_all(pieces, axis, split_axis=0, concat_axis=0, tiled=True)  4.94 us
    dot_general x6, matrix products, block_pass(): jnp.einsum('nt,hnp->thp', c_rows.astype(jnp.float32), start_state, precis...  4.21 us
  transfers between devices with their start and end apart: 5, of which 3 were waited for; matrix products, arithmetic and copies ran while one was open for 16% of the time, Pallas kernels for 0%

commit v1 on v0

v1 whole, which is shorter than its diff:
```python
import functools

import jax
import jax.numpy as jnp
from jax import lax
from jax.experimental import pallas as pl
from jax.experimental.pallas import tpu as pltpu
from jax.sharding import Mesh
from jax.sharding import PartitionSpec as P

MESH = pl.DeviceIdType.MESH
CTX = ("ctx_0", "ctx_1")
F32 = jnp.float32
BF16 = jnp.bfloat16
BLOCK = 256
LOG2E = 1.4426950408889634


def iota(shape, dim):
    return lax.broadcasted_iota(jnp.int32, shape, dim)


def dot(a, b):
    return jnp.dot(a, b, preferred_element_type=F32)


def far_first(n):
    return sorted(range(1, n), key=lambda k: -min(k, n - k))


def three_parts(a):
    hi = a.astype(BF16)
    rest = a - hi.astype(F32)
    mid = rest.astype(BF16)
    low = (rest - mid.astype(F32)).astype(BF16)
    return hi, mid, low


def running_sums(rows):
    until = (iota((BLOCK, BLOCK), 0) <= iota((BLOCK, BLOCK), 1)).astype(F32).astype(BF16)
    count = rows.shape[0]
    sums = dot(jnp.concatenate(three_parts(rows), axis=0), until)
    total = sums[:count] + (sums[count : 2 * count] + sums[2 * count :])
    return total * LOG2E


def log_gain(rows):
    z = 2.0 * rows
    series = 1.0 / 362880.0
    for factor in (40320.0, 5040.0, 720.0, 120.0, 24.0, 6.0, 2.0, 1.0):
        series = series * z + 1.0 / factor
    squared = jnp.where(z > -0.5, -z * series, 1.0 - jnp.exp(z))
    return jnp.where(squared > 0.0, (0.5 * LOG2E) * jnp.log(squared), -1e30)


def pair_of(even, odd, low_lanes):
    return jnp.where(low_lanes, even, odd)


def rows16(tile):
    return jnp.concatenate(
        [jnp.broadcast_to(tile[0:1], (16, 128)), jnp.broadcast_to(tile[1:2], (16, 128))], axis=0
    )


def pair_states(b_rows, weights, x_ref, unit_of, heads):
    low16 = iota((16, 128), 1) < 64
    found = []
    for group in range(heads // 4):
        push = jnp.concatenate(
            [b_rows * weights[4 * group + i : 4 * group + i + 1, :] for i in range(4)], axis=0
        ).astype(BF16)
        unit, lane = unit_of(group)
        sums = dot(push, x_ref[unit, :, lane : lane + 256])
        for i in range(2):
            part = sums[32 * i : 32 * i + 32, 128 * i : 128 * i + 128]
            found.append(pair_of(part[0:16], part[16:32], low16))
    return found


def store_parts(ref, index, lane, state):
    for place, part in enumerate(three_parts(state)):
        ref[index, 16 * place : 16 * place + 16, lane : lane + 128] = part


def kernel(
    nx, ny, nz,
    px, pbc, pld, bx, bbc, bld, bprompt, blen,
    py, by,
    xall, inner, lead, outs, scores, c_cols, b_pad, run_cols, q_rows, w_rows, e_rows,
    state_parts, mid_parts, start_parts,
    ysend, yrecv, back, decay, xsend, xrecv, before, final, hub_state, tile, prompts, staged, start,
    in_sem, out_sem, ys, yr, xs, xr, bs, br, fs, fr, ts, tr, gs, gr,
):
    x, y, p = lax.axis_index("ctx_0"), lax.axis_index("ctx_1"), lax.axis_index("pair")
    hub = (x * ny + y) // 2
    is_hub = p == hub
    not_hub = p != hub

    barrier = pltpu.get_barrier_semaphore()

    def greet(where):
        pl.semaphore_signal(barrier, inc=1, device_id=where, device_id_type=MESH)

    for k in range(1, ny):
        greet({"ctx_1": lax.rem(y + k, ny)})
    for k in range(1, nx):
        greet({"ctx_0": lax.rem(x + k, nx)})

    @pl.when(is_hub)
    def _():
        for k in range(1, nz):
            greet({"pair": lax.rem(p + k, nz)})

    @pl.when(not_hub)
    def _():
        greet({"pair": hub})

    def x_copy(u):
        if u < 4:
            source = px.at[u // 2, :, pl.ds(512 * (u % 2), 512)]
        else:
            source = bx.at[(u - 4) // 2, pl.ds(BLOCK * (u % 2), BLOCK), :]
        return pltpu.make_async_copy(source, xall.at[u], in_sem.at[u])

    for u in range(8):
        x_copy(u).start()

    low8 = iota((8, 128), 1) < 64

    rows = jnp.concatenate([pld[0], pld[1]], axis=0)
    run = running_sums(rows)
    q = run - log_gain(rows)
    run_end = run[:, BLOCK - 1 : BLOCK]
    weights = jnp.exp2(run_end - q)
    ends = jnp.broadcast_to(jnp.exp2(run_end), (32, 128))
    q_rows[0:32, :] = q
    for u in range(4):
        x_copy(u).wait()
    for pr in range(2):
        b_rows = pbc[0, pr].astype(F32)
        states = pair_states(
            b_rows,
            weights[16 * pr : 16 * pr + 16],
            xall,
            lambda group, pr=pr: (2 * pr + group // 2, 256 * (group % 2)),
            16,
        )
        for j in range(8):
            ysend[j, 16 * pr : 16 * pr + 16, :] = states[j]
    first_row = iota((8, 128), 0) == 0
    for j in range(8):
        per_prompt = [
            pair_of(
                jnp.broadcast_to(ends[16 * pr + 2 * j : 16 * pr + 2 * j + 1], (8, 128)),
                jnp.broadcast_to(ends[16 * pr + 2 * j + 1 : 16 * pr + 2 * j + 2], (8, 128)),
                low8,
            )
            for pr in range(2)
        ]
        ysend[j, 32:40, :] = jnp.where(first_row, per_prompt[0], per_prompt[1])
    tile[...] = jnp.full((8, 128), bprompt[0], jnp.int32).astype(F32)

    pl.semaphore_wait(barrier, ny - 1 + nx - 1 + 1 + (nz - 2) * is_hub.astype(jnp.int32))

    def y_copy(k):
        there = lax.rem(y + k, ny)
        return pltpu.make_async_remote_copy(
            src_ref=ysend.at[there], dst_ref=yrecv.at[k], send_sem=ys.at[k], recv_sem=yr.at[k],
            device_id={"ctx_1": there}, device_id_type=MESH,
        )

    for k in far_first(ny):
        y_copy(k).start()

    from_hub = lax.rem(p - hub + nz, nz)

    def tile_copy(k):
        return pltpu.make_async_remote_copy(
            src_ref=tile, dst_ref=prompts.at[k], send_sem=ts, recv_sem=tr.at[k],
            device_id={"pair": hub}, device_id_type=MESH,
        )

    @pl.when(not_hub)
    def _():
        tile_copy(from_hub).start()

    yrecv[0] = ysend[y]

    b_rows_in = [bld[b, :, BLOCK * k : BLOCK * k + BLOCK] for b in range(2) for k in range(2)]
    rows = jnp.concatenate(b_rows_in, axis=0)
    b_run = running_sums(rows)
    b_q = b_run - log_gain(rows)
    b_end = b_run[:, BLOCK - 1 : BLOCK]
    q_rows[32:64, :] = b_q
    w_rows[...] = jnp.exp2(b_end - b_q)
    e_rows[...] = jnp.broadcast_to(jnp.exp2(b_end), (32, 128))
    run_cols[...] = jnp.concatenate([run, b_run, jnp.zeros((64, BLOCK), F32)], axis=0).T
    for s in range(6):
        if s < 2:
            b_in, c_in = pbc[0, s], pbc[1, s]
        else:
            b, k = (s - 2) // 2, s % 2
            b_in = bbc[0, b, :, BLOCK * k : BLOCK * k + BLOCK]
            c_in = bbc[1, b, :, BLOCK * k : BLOCK * k + BLOCK]
        c_in = c_in.astype(F32)
        c_cols[s] = jnp.concatenate([c_in, c_in, c_in, jnp.zeros((80, BLOCK), F32)], axis=0).T.astype(BF16)
        b_pad[s, 0:16, :] = b_in
        b_pad[s, 16:128, :] = jnp.zeros((112, BLOCK), BF16)
    for ref in (state_parts, mid_parts, start_parts):
        for i in range(ref.shape[0]):
            ref[i, 48:128, :] = jnp.zeros((80, 512), BF16)

    low256 = iota((BLOCK, 128), 1) < 64
    causal = iota((BLOCK, BLOCK), 1) <= iota((BLOCK, BLOCK), 0)

    def unit_pass(u, carry):
        s = jnp.where(u < 4, u // 2, u - 2)
        scores[...] = jnp.where(causal, dot(c_cols[s], b_pad[s]), 0.0)
        cols = pltpu.roll(run_cols[...], lax.rem(128 - 8 * u, 128), 1)
        q_unit = q_rows[pl.ds(pl.multiple_of(8 * u, 8), 8), :]
        for j in range(4):
            x_pair = xall[u, :, 128 * j : 128 * j + 128]
            products, spread = [], []
            for h in (2 * j, 2 * j + 1):
                col = jnp.broadcast_to(cols[:, h : h + 1], (BLOCK, 128))
                row = q_unit[h : h + 1, :]
                upper = jnp.exp2(jnp.minimum(col[:128] - row[:, :128], 0.0)) * scores[0:128, 0:128]
                left = jnp.exp2(jnp.minimum(col[128:] - row[:, :128], 0.0)) * scores[128:256, 0:128]
                right = jnp.exp2(jnp.minimum(col[128:] - row[:, 128:], 0.0)) * scores[128:256, 128:256]
                top = dot(upper.astype(BF16), x_pair[:128])
                low = dot(jnp.concatenate([left, right], axis=1).astype(BF16), x_pair)
                products.append(jnp.concatenate([top, low], axis=0))
                spread.append(col)
            inner[u, :, 128 * j : 128 * j + 128] = pair_of(products[0], products[1], low256)
            lead[u, :, 128 * j : 128 * j + 128] = jnp.exp2(pair_of(spread[0], spread[1], low256))
        return carry

    lax.fori_loop(0, 4, unit_pass, 0)

    for k in range(1, ny):
        y_copy(k).wait_recv()
    state = jnp.zeros((32, 128), F32)
    fall = jnp.ones((8, 128), F32)
    for s in range(ny):
        slot = lax.rem(y - s + ny, ny)
        back[s] = state
        decay[s] = fall
        step = yrecv[slot, 32:40, :]
        state = rows16(step) * state + yrecv[slot, 0:32, :]
        fall = fall * step
    xsend[0:32, :] = state
    xsend[32:40, :] = fall

    def x_row_copy(k):
        there = lax.rem(x + k, nx)
        return pltpu.make_async_remote_copy(
            src_ref=xsend, dst_ref=xrecv.at[k], send_sem=xs.at[k], recv_sem=xr.at[k],
            device_id={"ctx_0": there}, device_id_type=MESH,
        )

    for k in far_first(nx):
        x_row_copy(k).start()
    xrecv[0] = xsend[...]

    for u in range(4, 8):
        x_copy(u).wait()
    lax.fori_loop(4, 6, unit_pass, 0)

    for k in range(1, nx):
        x_row_copy(k).wait_recv()
    state = jnp.zeros((32, 128), F32)
    mine = state
    for s in range(nx):
        slot = lax.rem(x - s + nx, nx)
        mine = jnp.where(x == s, state, mine)
        state = rows16(xrecv[slot, 32:40, :]) * state + xrecv[slot, 0:32, :]
    final[...] = state

    hub_y = lax.rem(2 * p + y // 4, ny)
    place = lax.rem(y, 4)
    sends_final = x == (2 * p) // ny

    def final_copy():
        return pltpu.make_async_remote_copy(
            src_ref=final, dst_ref=hub_state.at[place], send_sem=fs, recv_sem=fr.at[place],
            device_id={"ctx_1": hub_y}, device_id_type=MESH,
        )

    @pl.when(jnp.logical_and(sends_final, y != hub_y))
    def _():
        final_copy().start()

    @pl.when(jnp.logical_and(sends_final, y == hub_y))
    def _():
        pltpu.make_async_copy(final, hub_state.at[place], fr.at[place]).start()

    def back_copy(k):
        there = lax.rem(y + k, ny)
        return pltpu.make_async_remote_copy(
            src_ref=back.at[there], dst_ref=before.at[k], send_sem=bs.at[k], recv_sem=br.at[k],
            device_id={"ctx_1": there}, device_id_type=MESH,
        )

    for s in range(ny):
        back[s] = back[s] + rows16(decay[s]) * mine
    for k in far_first(ny):
        back_copy(k).start()
    before[0] = back[y]

    lax.fori_loop(6, 8, unit_pass, 0)

    def start_copy(k):
        there = lax.rem(p + k, nz)
        return pltpu.make_async_remote_copy(
            src_ref=staged.at[k], dst_ref=start, send_sem=gs.at[k], recv_sem=gr,
            device_id={"pair": there}, device_id_type=MESH,
        )

    @pl.when(is_hub)
    def _():
        for i in range(4):
            pltpu.make_async_copy(final, hub_state.at[i], fr.at[i]).wait()
        for k in range(1, nz):
            tile_copy(k).wait_recv()
        for k in far_first(nz):
            first = prompts[k] < 0.5
            first = jnp.concatenate([first, first], axis=0)
            for i in range(4):
                staged[k, 16 * i : 16 * i + 16, :] = jnp.where(
                    first, hub_state[i, 0:16, :], hub_state[i, 16:32, :]
                )
            start_copy(k).start()
        first = tile[...] < 0.5
        first = jnp.concatenate([first, first], axis=0)
        for i in range(4):
            start[16 * i : 16 * i + 16, :] = jnp.where(
                first, hub_state[i, 0:16, :], hub_state[i, 16:32, :]
            )

    low1 = iota((1, 128), 1) < 64
    for b in range(2):
        first, second = 4 + 2 * b, 5 + 2 * b
        states = pair_states(
            bbc[0, b, :, 0:BLOCK].astype(F32),
            w_rows[16 * b : 16 * b + 8],
            xall,
            lambda group, first=first: (first, 256 * group),
            8,
        )
        for j in range(4):
            store_parts(mid_parts, b, 128 * j, states[j])
        carried = dot(c_cols[3 + 2 * b], mid_parts[b])
        place_of = iota((BLOCK, 128), 0)
        for j in range(4):
            lanes = slice(128 * j, 128 * j + 128)
            fall = pair_of(e_rows[16 * b + 2 * j : 16 * b + 2 * j + 1], e_rows[16 * b + 2 * j + 1 : 16 * b + 2 * j + 2], low1)
            live = place_of < blen[b]
            inner[first, :, lanes] = jnp.where(live, inner[first, :, lanes], 0.0)
            lead[first, :, lanes] = jnp.where(live, lead[first, :, lanes], 0.0)
            live = place_of + BLOCK < blen[b]
            own = lead[second, :, lanes]
            inner[second, :, lanes] = jnp.where(live, inner[second, :, lanes] + own * carried[:, lanes], 0.0)
            lead[second, :, lanes] = jnp.where(live, own * fall, 0.0)

    def finish(u, parts):
        s = u // 2 if u < 4 else u - 2
        carried = dot(c_cols[s], parts)
        outs[u] = (inner[u] + lead[u] * carried).astype(BF16)
        out_copy(u).start()

    def out_copy(u):
        if u < 4:
            target = py.at[u // 2, :, pl.ds(512 * (u % 2), 512)]
        else:
            target = by.at[(u - 4) // 2, pl.ds(BLOCK * (u % 2), BLOCK), :]
        return pltpu.make_async_copy(outs.at[u], target, out_sem.at[u])

    for k in range(1, ny):
        back_copy(k).wait_recv()
    for j in range(8):
        slot = lax.rem(y - j + ny, ny)
        for pr in range(2):
            store_parts(state_parts, 2 * pr + j // 4, 128 * (j % 4), before[slot, 16 * pr : 16 * pr + 16, :])
    for u in range(4):
        finish(u, state_parts[u])

    @pl.when(not_hub)
    def _():
        start_copy(1).wait_recv()

    for i in range(4):
        store_parts(start_parts, 0, 128 * i, start[16 * i : 16 * i + 16, :])
    for u in range(4, 8):
        finish(u, start_parts[0])

    for k in range(1, ny):
        y_copy(k).wait_send()
        back_copy(k).wait_send()
    for k in range(1, nx):
        x_row_copy(k).wait_send()

    @pl.when(jnp.logical_and(sends_final, y != hub_y))
    def _():
        final_copy().wait_send()

    @pl.when(not_hub)
    def _():
        tile_copy(from_hub).wait_send()

    @pl.when(is_hub)
    def _():
        for k in range(1, nz):
            start_copy(k).wait_send()

    for u in range(8):
        out_copy(u).wait()


def body(nx, ny, nz, px, pbc, pld, bx, bbc, bld, bprompt, blen):
    any_space = pl.BlockSpec(memory_space=pl.ANY)
    vmem = pl.BlockSpec(memory_space=pltpu.VMEM)
    smem = pl.BlockSpec(memory_space=pltpu.SMEM)
    dma = pltpu.SemaphoreType.DMA
    return pl.pallas_call(
        functools.partial(kernel, nx, ny, nz),
        out_shape=(jax.ShapeDtypeStruct(px.shape, BF16), jax.ShapeDtypeStruct(bx.shape, BF16)),
        in_specs=[any_space, vmem, vmem, any_space, vmem, vmem, smem, smem],
        out_specs=(any_space, any_space),
        scratch_shapes=[
            pltpu.VMEM((8, BLOCK, 512), BF16),
            pltpu.VMEM((8, BLOCK, 512), F32),
            pltpu.VMEM((8, BLOCK, 512), F32),
            pltpu.VMEM((8, BLOCK, 512), BF16),
            pltpu.VMEM((BLOCK, BLOCK), F32),
            pltpu.VMEM((6, BLOCK, 128), BF16),
            pltpu.VMEM((6, 128, BLOCK), BF16),
            pltpu.VMEM((BLOCK, 128), F32),
            pltpu.VMEM((64, BLOCK), F32),
            pltpu.VMEM((32, BLOCK), F32),
            pltpu.VMEM((32, 128), F32),
            pltpu.VMEM((4, 128, 512), BF16),
            pltpu.VMEM((2, 128, 512), BF16),
            pltpu.VMEM((1, 128, 512), BF16),
            pltpu.VMEM((ny, 40, 128), F32),
            pltpu.VMEM((ny, 40, 128), F32),
            pltpu.VMEM((ny, 32, 128), F32),
            pltpu.VMEM((ny, 8, 128), F32),
            pltpu.VMEM((40, 128), F32),
            pltpu.VMEM((nx, 40, 128), F32),
            pltpu.VMEM((ny, 32, 128), F32),
            pltpu.VMEM((32, 128), F32),
            pltpu.VMEM((4, 32, 128), F32),
            pltpu.VMEM((8, 128), F32),
            pltpu.VMEM((nz, 8, 128), F32),
            pltpu.VMEM((nz, 64, 128), F32),
            pltpu.VMEM((64, 128), F32),
            dma((8,)), dma((8,)),
            dma((ny,)), dma((ny,)),
            dma((nx,)), dma((nx,)),
            dma((ny,)), dma((ny,)),
            dma, dma((4,)),
            dma, dma((nz,)),
            dma((nz,)), dma,
        ],
        compiler_params=pltpu.CompilerParams(collective_id=0, has_side_effects=True),
        name="layer",
    )(px, pbc, pld, bx, bbc, bld, bprompt, blen)


def solution(mesh):
    nx = 4
    ny, nz = mesh.shape["ctx"] // nx, mesh.shape["pair"]
    finer = Mesh(mesh.devices.reshape(nx, ny, nz), ("ctx_0", "ctx_1", "pair"))
    return jax.shard_map(
        functools.partial(body, nx, ny, nz),
        mesh=finer,
        in_specs=(
            P(None, CTX, "pair"),
            P(None, None, None, CTX),
            P(None, "pair", CTX),
            P("pair", None, CTX),
            P(None, "pair", None, None),
            P("pair", CTX, None),
            P("pair"),
            P("pair"),
        ),
        out_specs=(P(None, CTX, "pair"), P("pair", None, CTX)),
        check_vma=False,
    )
```

time: 166 us -> 40 us (0.24)
  the two profiles are of different devices: /device:TPU:7 before, /device:TPU:14 now
where the time goes in v1:
time: 40 us; the launch traced here: 39.8 us
  Pallas kernels  35.2 us (88%)
  local copies, waits for them, and re-layouts  3.32 us (8%)
  between operations  1.3 us (3%)
    pallas_call x1, Pallas kernels, body(): pl.pallas_call(functools.partial(kernel, nx, ny, nz), out_shape=(jax.Shap...  35.2 us
    unnamed x4, local copies, waits for them, and re-layouts  3.32 us

profile of v1, /device:TPU:14, one launch (start us, length us, event | category | flops | bytes accessed | tf_op | source)
XLA Modules:
  0.0 39.8 jit_solution(8743660286870568024)
XLA Ops:
  1.3 35.2 %layer.1 = (bf16[2,256,1024]{2,1,0:T(8,128)(2,1)}, bf16[2,512,512]{2,1,0:T(8,128)(2,1)}) custom-call(bf16[2,256,1024]{2,1,0:T(8,128)(2,1)} %px.1, bf16[2,2,16,256]{3,2,1,0:T(8,128)(2,1)} %pbc.1, f32[2,16,256]{2,1,0:T(8,128)} %pld.1, bf16[2,512,512]{2,1,0:T(8,128)(2,1)} %bx.1, bf16[2,2,16,512]{3,2,1,0:T(8,128)(2,1)} %bbc.1, f32[2,8,512]{2,1,0:T(8,128)} %bld.1, ...), custom_call_target="tpu_custom_call" | custom-call | tf_op jit(solution)/shard_map/layer/pallas_call | solution.py:425
  36.5 0.0 copy-start
  36.5 2.4 %copy.13 = bf16[2,256,1024]{2,1,0:T(8,128)(2,1)} copy(bf16[2,256,1024]{2,1,0:T(8,128)(2,1)} %get-tuple-element.4) | data formatting | bytes 2097152
  38.8 0.0 copy-done
  38.8 1.0 %copy.14 = bf16[2,512,512]{2,1,0:T(8,128)(2,1)} copy(bf16[2,512,512]{2,1,0:T(8,128)(2,1)S(1)} %copy-done) | data formatting | bytes 2097152
Async XLA Ops:
  36.5 2.4 %copy-start = (bf16[2,512,512]{2,1,0:T(8,128)(2,1)S(1)}, bf16[2,512,512]{2,1,0:T(8,128)(2,1)}, u32[]{:S(2)}) copy-start(bf16[2,512,512]{2,1,0:T(8,128)(2,1)} %get-tuple-element.5) | copy-start | bytes 3145732

commit v2 on v1

v2 whole, which is shorter than its diff:
```python
import functools

import jax
import jax.numpy as jnp
from jax import lax
from jax.experimental import pallas as pl
from jax.experimental.pallas import tpu as pltpu
from jax.sharding import Mesh
from jax.sharding import PartitionSpec as P

MESH = pl.DeviceIdType.MESH
CTX = ("ctx_0", "ctx_1")
F32 = jnp.float32
BF16 = jnp.bfloat16
BLOCK = 256
LOG2E = 1.4426950408889634
FIRST_PART = 6
SECOND_PART = 8


def iota(shape, dim):
    return lax.broadcasted_iota(jnp.int32, shape, dim)


def dot(a, b):
    return jnp.dot(a, b, preferred_element_type=F32)


def far_first(n):
    return sorted(range(1, n), key=lambda k: -min(k, n - k))


def three_parts(a):
    hi = a.astype(BF16)
    rest = a - hi.astype(F32)
    mid = rest.astype(BF16)
    low = (rest - mid.astype(F32)).astype(BF16)
    return hi, mid, low


def running_sums(rows):
    until = (iota((BLOCK, BLOCK), 0) <= iota((BLOCK, BLOCK), 1)).astype(F32).astype(BF16)
    count = rows.shape[0]
    sums = dot(jnp.concatenate(three_parts(rows), axis=0), until)
    total = sums[:count] + (sums[count : 2 * count] + sums[2 * count :])
    return total * LOG2E


def log_gain(rows):
    z = 2.0 * rows
    series = 1.0 / 362880.0
    for factor in (40320.0, 5040.0, 720.0, 120.0, 24.0, 6.0, 2.0, 1.0):
        series = series * z + 1.0 / factor
    squared = jnp.where(z > -0.5, -z * series, 1.0 - jnp.exp(z))
    return jnp.where(squared > 0.0, (0.5 * LOG2E) * jnp.log(squared), -1e30)


def pair_of(even, odd, low_lanes):
    return jnp.where(low_lanes, even, odd)


def rows16(tile):
    return jnp.concatenate(
        [jnp.broadcast_to(tile[0:1], (16, 128)), jnp.broadcast_to(tile[1:2], (16, 128))], axis=0
    )


def pair_states(b_rows, weights, x_ref, unit_of, heads):
    low16 = iota((16, 128), 1) < 64
    found = []
    for group in range(heads // 4):
        push = jnp.concatenate(
            [b_rows * weights[4 * group + i : 4 * group + i + 1, :] for i in range(4)], axis=0
        ).astype(BF16)
        unit, lane = unit_of(group)
        sums = dot(push, x_ref[unit, :, lane : lane + 256])
        for i in range(2):
            part = sums[32 * i : 32 * i + 32, 128 * i : 128 * i + 128]
            found.append(pair_of(part[0:16], part[16:32], low16))
    return found


def store_parts(ref, lane, state):
    for place, part in enumerate(three_parts(state)):
        ref[16 * place : 16 * place + 16, lane : lane + 128] = part


def kernel(
    nx, ny, nz,
    px, pbc_in, pld_in, bx, bbc_in, bld_in, blen_in, bprompt,
    prompt_outs, b_inner, b_lead, start_parts, b_cols,
    pbc, pld, bbc, bld, blen,
    xall, p_inner, p_lead, scores, c_cols, b_pad, run_cols, q_rows, w_rows, e_rows,
    state_parts, mid_parts,
    ysend, yfall, yrecv, yfell, back, decay, xsend, xfall, xrecv, xfell, before, row_in, row_fell,
    tile, prompts, staged, start,
    in_sem, ys, yr, ds, dr, xs, xr, es, er, bs, br, fs, fr, ts, tr, gs, gr,
):
    x, y, p = lax.axis_index("ctx_0"), lax.axis_index("ctx_1"), lax.axis_index("pair")
    hub = (x * ny + y) // 2
    is_hub = p == hub
    not_hub = p != hub

    barrier = pltpu.get_barrier_semaphore()

    def greet(where):
        pl.semaphore_signal(barrier, inc=1, device_id=where, device_id_type=MESH)

    first_hub = lax.rem(2 * p, ny)

    def holder(j):
        return lax.rem(first_hub + ny + (j - 3 if j >= 4 else -j), ny)

    def held_by(at):
        far = lax.rem(at - first_hub + ny, ny)
        return jnp.where(jnp.logical_and(far >= 1, far <= 4), far + 3, lax.rem(ny - far, ny))

    mine_j = held_by(y)
    place = lax.rem(mine_j, 4)
    hub_x = (2 * p) // ny
    hub_y = lax.rem(first_hub + mine_j // 4, ny)
    other_row = x != hub_x
    at_hub = jnp.logical_and(x == hub_x, y == hub_y)
    from_hub = jnp.logical_not(at_hub)
    for k in range(1, ny):
        greet({"ctx_1": lax.rem(y + k, ny)})
    for k in range(1, nx):
        greet({"ctx_0": lax.rem(x + k, nx)})

    @pl.when(is_hub)
    def _():
        for k in range(1, nz):
            greet({"pair": lax.rem(p + k, nz)})
        side = 2 * (y - first_hub) - 1
        for k in range(1, nx):
            for i in range(4):
                greet({"ctx_0": lax.rem(x + k, nx), "ctx_1": lax.rem(y + side * i + ny, ny)})

    @pl.when(other_row)
    def _():
        greet({"ctx_0": hub_x, "ctx_1": hub_y})

    @pl.when(not_hub)
    def _():
        greet({"pair": hub})

    small = [
        pltpu.make_async_copy(source, target, in_sem.at[8 + i])
        for i, (source, target) in enumerate(
            [(pld_in, pld), (pbc_in, pbc), (bld_in, bld), (bbc_in, bbc), (blen_in, blen)]
        )
    ]

    def x_copy(u):
        if u < 4:
            source = px.at[u // 2, :, pl.ds(512 * (u % 2), 512)]
        else:
            source = bx.at[(u - 4) // 2, pl.ds(BLOCK * (u % 2), BLOCK), :]
        return pltpu.make_async_copy(source, xall.at[u], in_sem.at[u])

    small[0].start()
    small[1].start()
    for u in range(4):
        x_copy(u).start()
    for copy in small[2:]:
        copy.start()
    for u in range(4, 8):
        x_copy(u).start()

    def y_copy(pr, k):
        there = lax.rem(y + k, ny)
        return pltpu.make_async_remote_copy(
            src_ref=ysend.at[pr, held_by(there)], dst_ref=yrecv.at[pr, k],
            send_sem=ys.at[ny * pr + k], recv_sem=yr.at[ny * pr + k],
            device_id={"ctx_1": there}, device_id_type=MESH,
        )

    def fall_copy(k):
        there = lax.rem(y + k, ny)
        return pltpu.make_async_remote_copy(
            src_ref=yfall.at[held_by(there)], dst_ref=yfell.at[k], send_sem=ds.at[k], recv_sem=dr.at[k],
            device_id={"ctx_1": there}, device_id_type=MESH,
        )

    def tile_copy(of):
        return pltpu.make_async_remote_copy(
            src_ref=tile, dst_ref=prompts.at[of], send_sem=ts, recv_sem=tr.at[of],
            device_id={"pair": hub}, device_id_type=MESH,
        )

    low8 = iota((8, 128), 1) < 64

    small[0].wait()
    rows = jnp.concatenate([pld[0], pld[1]], axis=0)
    run = running_sums(rows)
    q = run - log_gain(rows)
    run_end = run[:, BLOCK - 1 : BLOCK]
    weights = jnp.exp2(run_end - q)
    ends = jnp.broadcast_to(jnp.exp2(run_end), (32, 128))
    q_rows[0:32, :] = q
    low1 = iota((1, 128), 1) < 64
    for pr in range(2):
        for j in range(8):
            h = 16 * pr + 2 * j
            yfall[j, pr : pr + 1, :] = pair_of(ends[h : h + 1], ends[h + 1 : h + 2], low1)
    small[1].wait()
    for pr in range(2):
        x_copy(2 * pr).wait()
        x_copy(2 * pr + 1).wait()
        states = pair_states(
            pbc[0, pr].astype(F32),
            weights[16 * pr : 16 * pr + 16],
            xall,
            lambda group, pr=pr: (2 * pr + group // 2, 256 * (group % 2)),
            16,
        )
        for j in range(8):
            ysend[pr, j] = states[j]
        if pr == 0:
            more = (nz - 2 + 4 * (nx - 1)) * is_hub.astype(jnp.int32) + other_row.astype(jnp.int32)
            pl.semaphore_wait(barrier, ny - 1 + nx - 1 + 1 + more)
        for k in far_first(ny):
            y_copy(pr, k).start()
    for k in far_first(ny):
        fall_copy(k).start()
    tile[...] = jnp.full((8, 128), bprompt[0], jnp.int32).astype(F32)

    @pl.when(not_hub)
    def _():
        tile_copy(p).start()

    for pr in range(2):
        yrecv[pr, 0] = ysend[pr, mine_j]
    yfell[0] = yfall[mine_j]

    small[2].wait()
    small[3].wait()
    b_rows_in = [bld[b, :, BLOCK * k : BLOCK * k + BLOCK] for b in range(2) for k in range(2)]
    rows = jnp.concatenate(b_rows_in, axis=0)
    b_run = running_sums(rows)
    b_q = b_run - log_gain(rows)
    b_end = b_run[:, BLOCK - 1 : BLOCK]
    q_rows[32:64, :] = b_q
    w_rows[...] = jnp.exp2(b_end - b_q)
    e_rows[...] = jnp.broadcast_to(jnp.exp2(b_end), (32, 128))
    run_cols[...] = jnp.concatenate([run, b_run, jnp.zeros((64, BLOCK), F32)], axis=0).T
    for s in range(6):
        if s < 2:
            b_in, c_in = pbc[0, s], pbc[1, s]
        else:
            b, k = (s - 2) // 2, s % 2
            b_in = bbc[0, b, :, BLOCK * k : BLOCK * k + BLOCK]
            c_in = bbc[1, b, :, BLOCK * k : BLOCK * k + BLOCK]
        c_in = c_in.astype(F32)
        cols = jnp.concatenate([c_in, c_in, c_in, jnp.zeros((80, BLOCK), F32)], axis=0).T.astype(BF16)
        c_cols[s] = cols
        if s >= 2:
            b_cols[s - 2] = cols
        b_pad[s, 0:16, :] = b_in
        b_pad[s, 16:128, :] = jnp.zeros((112, BLOCK), BF16)
    start_parts[48:128, :] = jnp.zeros((80, 512), BF16)
    for ref in (state_parts, mid_parts):
        for i in range(ref.shape[0]):
            ref[i, 48:128, :] = jnp.zeros((80, 512), BF16)

    low256 = iota((BLOCK, 128), 1) < 64
    causal = iota((BLOCK, BLOCK), 1) <= iota((BLOCK, BLOCK), 0)

    def unit_pass(inner, lead, base, u, carry):
        s = jnp.where(u < 4, u // 2, u - 2)
        scores[...] = jnp.where(causal, dot(c_cols[s], b_pad[s]), 0.0)
        cols = pltpu.roll(run_cols[...], lax.rem(128 - 8 * u, 128), 1)
        q_unit = q_rows[pl.ds(pl.multiple_of(8 * u, 8), 8), :]
        for j in range(4):
            x_pair = xall[u, :, 128 * j : 128 * j + 128]
            products, spread = [], []
            for h in (2 * j, 2 * j + 1):
                col = jnp.broadcast_to(cols[:, h : h + 1], (BLOCK, 128))
                row = q_unit[h : h + 1, :]
                upper = jnp.exp2(jnp.minimum(col[:128] - row[:, :128], 0.0)) * scores[0:128, 0:128]
                left = jnp.exp2(jnp.minimum(col[128:] - row[:, :128], 0.0)) * scores[128:256, 0:128]
                right = jnp.exp2(jnp.minimum(col[128:] - row[:, 128:], 0.0)) * scores[128:256, 128:256]
                top = dot(upper.astype(BF16), x_pair[:128])
                low = dot(jnp.concatenate([left, right], axis=1).astype(BF16), x_pair)
                products.append(jnp.concatenate([top, low], axis=0))
                spread.append(col)
            inner[u - base, :, 128 * j : 128 * j + 128] = pair_of(products[0], products[1], low256)
            lead[u - base, :, 128 * j : 128 * j + 128] = jnp.exp2(pair_of(spread[0], spread[1], low256))
        return carry

    b_pass = functools.partial(unit_pass, b_inner, b_lead, 4)
    lax.fori_loop(0, 4, functools.partial(unit_pass, p_inner, p_lead, 0), 0)
    for u in range(4, 8):
        x_copy(u).wait()
    lax.fori_loop(4, FIRST_PART, b_pass, 0)

    for k in range(1, ny):
        fall_copy(k).wait_recv()
        for pr in range(2):
            y_copy(pr, k).wait_recv()
    state = [jnp.zeros((16, 128), F32)] * 2
    fall = jnp.ones((2, 128), F32)
    for s in range(ny):
        slot = lax.rem(y - s + ny, ny)
        decay[s] = fall
        step = yfell[slot]
        for pr in range(2):
            back[s, 16 * pr : 16 * pr + 16, :] = state[pr]
            state[pr] = step[pr : pr + 1] * state[pr] + yrecv[pr, slot]
        fall = fall * step
    for pr in range(2):
        xsend[16 * pr : 16 * pr + 16, :] = state[pr]
    xfall[...] = fall

    def x_row_copy(k):
        there = lax.rem(x + k, nx)
        return pltpu.make_async_remote_copy(
            src_ref=xsend, dst_ref=xrecv.at[k], send_sem=xs.at[k], recv_sem=xr.at[k],
            device_id={"ctx_0": there}, device_id_type=MESH,
        )

    def x_fall_copy(k):
        there = lax.rem(x + k, nx)
        return pltpu.make_async_remote_copy(
            src_ref=xfall, dst_ref=xfell.at[k], send_sem=es.at[k], recv_sem=er.at[k],
            device_id={"ctx_0": there}, device_id_type=MESH,
        )

    def total_copy():
        return pltpu.make_async_remote_copy(
            src_ref=xsend, dst_ref=row_in.at[x, place], send_sem=fs.at[0], recv_sem=fr.at[0, 4 * x + place],
            device_id={"ctx_0": hub_x, "ctx_1": hub_y}, device_id_type=MESH,
        )

    def total_fall_copy():
        return pltpu.make_async_remote_copy(
            src_ref=xfall, dst_ref=row_fell.at[x, place], send_sem=fs.at[1], recv_sem=fr.at[1, 4 * x + place],
            device_id={"ctx_0": hub_x, "ctx_1": hub_y}, device_id_type=MESH,
        )

    @pl.when(from_hub)
    def _():
        total_copy().start()
        total_fall_copy().start()

    @pl.when(at_hub)
    def _():
        pltpu.make_async_copy(xsend, row_in.at[x, place], fr.at[0, 4 * x + place]).start()
        pltpu.make_async_copy(xfall, row_fell.at[x, place], fr.at[1, 4 * x + place]).start()

    for k in far_first(nx):
        x_row_copy(k).start()
        x_fall_copy(k).start()
    xrecv[0] = xsend[...]
    xfell[0] = xfall[...]

    lax.fori_loop(FIRST_PART, SECOND_PART, b_pass, 0)

    for k in range(1, nx):
        x_fall_copy(k).wait_recv()
        x_row_copy(k).wait_recv()
    state = jnp.zeros((32, 128), F32)
    mine = state
    for s in range(nx):
        mine = jnp.where(x == s, state, mine)
        if s < nx - 1:
            slot = lax.rem(x - s + nx, nx)
            state = rows16(xfell[slot]) * state + xrecv[slot]

    def back_copy(k):
        there = lax.rem(y + k, ny)
        return pltpu.make_async_remote_copy(
            src_ref=back.at[there], dst_ref=before.at[k], send_sem=bs.at[k], recv_sem=br.at[k],
            device_id={"ctx_1": there}, device_id_type=MESH,
        )

    for s in range(ny):
        back[s] = back[s] + rows16(decay[s]) * mine
    for k in far_first(ny):
        back_copy(k).start()
    before[0] = back[y]

    lax.fori_loop(SECOND_PART, 8, b_pass, 0)

    def start_copy(to):
        return pltpu.make_async_remote_copy(
            src_ref=staged.at[to], dst_ref=start, send_sem=gs.at[to], recv_sem=gr,
            device_id={"pair": to}, device_id_type=MESH,
        )

    def chosen(flags, states):
        first = jnp.concatenate([flags, flags], axis=0) < 0.5
        return [jnp.where(first, state[0:16], state[16:32]) for state in states]

    @pl.when(is_hub)
    def _():
        states = []
        for i in range(4):
            state = jnp.zeros((32, 128), F32)
            for s in range(nx):
                pltpu.make_async_copy(xsend, row_in.at[s, i], fr.at[0, 4 * s + i]).wait()
                pltpu.make_async_copy(xfall, row_fell.at[s, i], fr.at[1, 4 * s + i]).wait()
                state = rows16(row_fell[s, i]) * state + row_in[s, i]
            states.append(state)
        for to in range(nz):

            @pl.when(p != to)
            def _(to=to):
                tile_copy(to).wait_recv()
                for i, state in enumerate(chosen(prompts[to], states)):
                    staged[to, 16 * i : 16 * i + 16, :] = state
                start_copy(to).start()

        for i, state in enumerate(chosen(tile[...], states)):
            start[16 * i : 16 * i + 16, :] = state

    small[4].wait()
    for b in range(2):
        first, second = 2 * b, 2 * b + 1
        states = pair_states(
            bbc[0, b, :, 0:BLOCK].astype(F32),
            w_rows[16 * b : 16 * b + 8],
            xall,
            lambda group, b=b: (4 + 2 * b, 256 * group),
            8,
        )
        for j in range(4):
            store_parts(mid_parts.at[b], 128 * j, states[j])
        carried = dot(c_cols[3 + 2 * b], mid_parts[b])
        place_of = iota((BLOCK, 128), 0)
        for j in range(4):
            lanes = slice(128 * j, 128 * j + 128)
            fall = pair_of(e_rows[16 * b + 2 * j : 16 * b + 2 * j + 1], e_rows[16 * b + 2 * j + 1 : 16 * b + 2 * j + 2], low1)
            live = place_of < blen[b]
            b_inner[first, :, lanes] = jnp.where(live, b_inner[first, :, lanes], 0.0)
            b_lead[first, :, lanes] = jnp.where(live, b_lead[first, :, lanes], 0.0)
            live = place_of + BLOCK < blen[b]
            own = b_lead[second, :, lanes]
            b_inner[second, :, lanes] = jnp.where(live, b_inner[second, :, lanes] + own * carried[:, lanes], 0.0)
            b_lead[second, :, lanes] = jnp.where(live, own * fall, 0.0)

    for k in range(1, ny):
        back_copy(k).wait_recv()
    for j in range(8):
        slot = lax.rem(y - holder(j) + ny, ny)
        for pr in range(2):
            store_parts(
                state_parts.at[2 * pr + j // 4], 128 * (j % 4), before[slot, 16 * pr : 16 * pr + 16, :]
            )
    for u in range(4):
        carried = dot(c_cols[u // 2], state_parts[u])
        prompt_outs[u] = (p_inner[u] + p_lead[u] * carried).astype(BF16)

    for k in range(1, ny):
        for pr in range(2):
            y_copy(pr, k).wait_send()
        fall_copy(k).wait_send()
        back_copy(k).wait_send()
    for k in range(1, nx):
        x_row_copy(k).wait_send()
        x_fall_copy(k).wait_send()

    @pl.when(from_hub)
    def _():
        total_copy().wait_send()
        total_fall_copy().wait_send()

    @pl.when(not_hub)
    def _():
        tile_copy(p).wait_send()
        start_copy(0).wait_recv()

    for i in range(4):
        store_parts(start_parts, 128 * i, start[16 * i : 16 * i + 16, :])

    @pl.when(is_hub)
    def _():
        for to in range(nz):

            @pl.when(p != to)
            def _(to=to):
                start_copy(to).wait_send()


def write_kernel(prompt_outs, b_inner, b_lead, start_parts, b_cols, py, by, outs, sem):
    copies = [
        pltpu.make_async_copy(prompt_outs.at[u], py.at[u // 2, :, pl.ds(512 * (u % 2), 512)], sem.at[u])
        for u in range(4)
    ]
    for copy in copies:
        copy.start()
    for u in range(4):
        outs[u] = (b_inner[u] + b_lead[u] * dot(b_cols[u], start_parts[...])).astype(BF16)
        copy = pltpu.make_async_copy(
            outs.at[u], by.at[u // 2, pl.ds(BLOCK * (u % 2), BLOCK), :], sem.at[4 + u]
        )
        copy.start()
        copies.append(copy)
    for copy in copies:
        copy.wait()


def body(nx, ny, nz, px, pbc, pld, bx, bbc, bld, bprompt, blen):
    any_space = pl.BlockSpec(memory_space=pl.ANY)
    vmem = pl.BlockSpec(memory_space=pltpu.VMEM)
    dma = pltpu.SemaphoreType.DMA
    between = [
        pltpu.VMEM((4, BLOCK, 512), BF16),
        pltpu.VMEM((4, BLOCK, 512), F32),
        pltpu.VMEM((4, BLOCK, 512), F32),
        pltpu.VMEM((128, 512), BF16),
        pltpu.VMEM((4, BLOCK, 128), BF16),
    ]
    kept = pl.pallas_call(
        functools.partial(kernel, nx, ny, nz),
        out_shape=between,
        in_specs=[pl.BlockSpec(memory_space=pltpu.HBM)] * 7 + [pl.BlockSpec(memory_space=pltpu.SMEM)],
        out_specs=[vmem] * 5,
        scratch_shapes=[
            pltpu.VMEM(pbc.shape, BF16),
            pltpu.VMEM(pld.shape, F32),
            pltpu.VMEM(bbc.shape, BF16),
            pltpu.VMEM(bld.shape, F32),
            pltpu.SMEM(blen.shape, jnp.int32),
            pltpu.VMEM((8, BLOCK, 512), BF16),
            pltpu.VMEM((4, BLOCK, 512), F32),
            pltpu.VMEM((4, BLOCK, 512), F32),
            pltpu.VMEM((BLOCK, BLOCK), F32),
            pltpu.VMEM((6, BLOCK, 128), BF16),
            pltpu.VMEM((6, 128, BLOCK), BF16),
            pltpu.VMEM((BLOCK, 128), F32),
            pltpu.VMEM((64, BLOCK), F32),
            pltpu.VMEM((32, BLOCK), F32),
            pltpu.VMEM((32, 128), F32),
            pltpu.VMEM((4, 128, 512), BF16),
            pltpu.VMEM((2, 128, 512), BF16),
            pltpu.VMEM((2, ny, 16, 128), F32),
            pltpu.VMEM((ny, 2, 128), F32),
            pltpu.VMEM((2, ny, 16, 128), F32),
            pltpu.VMEM((ny, 2, 128), F32),
            pltpu.VMEM((ny, 32, 128), F32),
            pltpu.VMEM((ny, 2, 128), F32),
            pltpu.VMEM((32, 128), F32),
            pltpu.VMEM((2, 128), F32),
            pltpu.VMEM((nx, 32, 128), F32),
            pltpu.VMEM((nx, 2, 128), F32),
            pltpu.VMEM((ny, 32, 128), F32),
            pltpu.VMEM((nx, 4, 32, 128), F32),
            pltpu.VMEM((nx, 4, 2, 128), F32),
            pltpu.VMEM((8, 128), F32),
            pltpu.VMEM((nz, 8, 128), F32),
            pltpu.VMEM((nz, 64, 128), F32),
            pltpu.VMEM((64, 128), F32),
            dma((13,)),
            dma((2 * ny,)), dma((2 * ny,)),
            dma((ny,)), dma((ny,)),
            dma((nx,)), dma((nx,)),
            dma((nx,)), dma((nx,)),
            dma((ny,)), dma((ny,)),
            dma((2,)), dma((2, 4 * nx)),
            dma, dma((nz,)),
            dma((nz,)), dma,
        ],
        compiler_params=pltpu.CompilerParams(
            collective_id=0, has_side_effects=True, vmem_limit_bytes=40 * 1024 * 1024
        ),
        name="layer",
    )(*[pltpu.with_memory_space_constraint(a, pltpu.HBM) for a in (px, pbc, pld, bx, bbc, bld, blen)], bprompt)
    return pl.pallas_call(
        write_kernel,
        out_shape=(jax.ShapeDtypeStruct(px.shape, BF16), jax.ShapeDtypeStruct(bx.shape, BF16)),
        in_specs=[vmem] * 5,
        out_specs=(any_space, any_space),
        scratch_shapes=[pltpu.VMEM((4, BLOCK, 512), BF16), dma((8,))],
        compiler_params=pltpu.CompilerParams(vmem_limit_bytes=16 * 1024 * 1024),
        name="write",
    )(*kept)


def solution(mesh):
    nx = 4
    ny, nz = mesh.shape["ctx"] // nx, mesh.shape["pair"]
    finer = Mesh(mesh.devices.reshape(nx, ny, nz), ("ctx_0", "ctx_1", "pair"))
    return jax.shard_map(
        functools.partial(body, nx, ny, nz),
        mesh=finer,
        in_specs=(
            P(None, CTX, "pair"),
            P(None, None, None, CTX),
            P(None, "pair", CTX),
            P("pair", None, CTX),
            P(None, "pair", None, None),
            P("pair", CTX, None),
            P("pair"),
            P("pair"),
        ),
        out_specs=(P(None, CTX, "pair"), P("pair", None, CTX)),
        check_vma=False,
    )
```

time: 40 us -> 33.3 us (0.83)
  the two profiles are of different devices: /device:TPU:14 before, /device:TPU:7 now
where the time goes in v2:
time: 33.3 us; the launch traced here: 33.2 us
  Pallas kernels  31.9 us (96%)
  between operations  1.29 us (4%)
    pallas_call x1, Pallas kernels, body(): pl.pallas_call(functools.partial(kernel, nx, ny, nz), out_shape=between,...  30.5 us
    pallas_call x1, Pallas kernels, body(): pl.pallas_call(write_kernel, out_shape=(jax.ShapeDtypeStruct(px.shape, BF...  1.39 us

profile of v2, /device:TPU:7, one launch (start us, length us, event | category | flops | bytes accessed | tf_op | source)
XLA Modules:
  0.0 33.2 jit_solution(6136769598579642509)
XLA Ops:
  1.3 30.5 %layer.1 = (bf16[4,256,512]{2,1,0:T(8,128)(2,1)S(1)}, f32[4,256,512]{2,1,0:T(8,128)S(1)}, f32[4,256,512]{2,1,0:T(8,128)S(1)}, bf16[128,512]{1,0:T(8,128)(2,1)S(1)}, bf16[4,256,128]{2,1,0:T(8,128)(2,1)S(1)}) custom-call(bf16[2,256,1024]{2,1,0:T(8,128)(2,1)} %px.1, bf16[2,2,16,256]{3,2,1,0:T(8,128)(2,1)} %pbc_in.1, f32[2,16,256]{2,1,0:T(8,128)} %pld_in.1, ...), custom_call_target="tpu_custom_call" | custom-call | tf_op jit(solution)/shard_map/layer/pallas_call | solution.py:514
  31.8 1.4 %write.1 = (bf16[2,256,1024]{2,1,0:T(8,128)(2,1)}, bf16[2,512,512]{2,1,0:T(8,128)(2,1)}) custom-call(bf16[4,256,512]{2,1,0:T(8,128)(2,1)S(1)} %get-tuple-element.7.prompt_outs, f32[4,256,512]{2,1,0:T(8,128)S(1)} %get-tuple-element.8.b_inner, f32[4,256,512]{2,1,0:T(8,128)S(1)} %get-tuple-element.9.b_lead, bf16[128,512]{1,0:T(8,128)(2,1)S(1)} %get-tuple-element.10.start_parts, ...), custom_call_target="tpu_custom_call" | custom-call | tf_op jit(solution)/shard_map/write/pallas_call | solution.py:569

commit v3 on v2

--- a/solution.py
+++ b/solution.py
@@ -14,8 +14,6 @@
 BF16 = jnp.bfloat16
 BLOCK = 256
 LOG2E = 1.4426950408889634
-FIRST_PART = 6
-SECOND_PART = 8
 
 
 def iota(shape, dim):
@@ -78,6 +76,10 @@
             part = sums[32 * i : 32 * i + 32, 128 * i : 128 * i + 128]
             found.append(pair_of(part[0:16], part[16:32], low16))
     return found
+
+
+def wait_for(ref, sem):
+    pltpu.make_async_copy(ref, ref, sem).wait()
 
 
 def store_parts(ref, lane, state):
@@ -145,7 +147,7 @@
         greet({"pair": hub})
 
     small = [
-        pltpu.make_async_copy(source, target, in_sem.at[8 + i])
+        pltpu.make_async_copy(source, target, in_sem.at[3 + i])
         for i, (source, target) in enumerate(
             [(pld_in, pld), (pbc_in, pbc), (bld_in, bld), (bbc_in, bbc), (blen_in, blen)]
         )
@@ -156,7 +158,7 @@
             source = px.at[u // 2, :, pl.ds(512 * (u % 2), 512)]
         else:
             source = bx.at[(u - 4) // 2, pl.ds(BLOCK * (u % 2), BLOCK), :]
-        return pltpu.make_async_copy(source, xall.at[u], in_sem.at[u])
+        return pltpu.make_async_copy(source, xall.at[u], in_sem.at[min(u // 2, 2)])
 
     small[0].start()
     small[1].start()
@@ -171,20 +173,20 @@
         there = lax.rem(y + k, ny)
         return pltpu.make_async_remote_copy(
             src_ref=ysend.at[pr, held_by(there)], dst_ref=yrecv.at[pr, k],
-            send_sem=ys.at[ny * pr + k], recv_sem=yr.at[ny * pr + k],
+            send_sem=ys, recv_sem=yr,
             device_id={"ctx_1": there}, device_id_type=MESH,
         )
 
     def fall_copy(k):
         there = lax.rem(y + k, ny)
         return pltpu.make_async_remote_copy(
-            src_ref=yfall.at[held_by(there)], dst_ref=yfell.at[k], send_sem=ds.at[k], recv_sem=dr.at[k],
+            src_ref=yfall.at[held_by(there)], dst_ref=yfell.at[k], send_sem=ds, recv_sem=dr,
             device_id={"ctx_1": there}, device_id_type=MESH,
         )
 
     def tile_copy(of):
         return pltpu.make_async_remote_copy(
-            src_ref=tile, dst_ref=prompts.at[of], send_sem=ts, recv_sem=tr.at[of],
+            src_ref=tile, dst_ref=prompts.at[of], send_sem=ts, recv_sem=tr,
             device_id={"pair": hub}, device_id_type=MESH,
         )
 
@@ -205,8 +207,7 @@
             yfall[j, pr : pr + 1, :] = pair_of(ends[h : h + 1], ends[h + 1 : h + 2], low1)
     small[1].wait()
     for pr in range(2):
-        x_copy(2 * pr).wait()
-        x_copy(2 * pr + 1).wait()
+        wait_for(xall.at[pl.ds(2 * pr, 2)], in_sem.at[pr])
         states = pair_states(
             pbc[0, pr].astype(F32),
             weights[16 * pr : 16 * pr + 16],
@@ -290,14 +291,11 @@
 
     b_pass = functools.partial(unit_pass, b_inner, b_lead, 4)
     lax.fori_loop(0, 4, functools.partial(unit_pass, p_inner, p_lead, 0), 0)
-    for u in range(4, 8):
-        x_copy(u).wait()
-    lax.fori_loop(4, FIRST_PART, b_pass, 0)
-
-    for k in range(1, ny):
-        fall_copy(k).wait_recv()
-        for pr in range(2):
-            y_copy(pr, k).wait_recv()
+    wait_for(xall.at[pl.ds(4, 4)], in_sem.at[2])
+    lax.fori_loop(4, 8, b_pass, 0)
+
+    wait_for(yfell.at[pl.ds(1, ny - 1)], dr)
+    wait_for(yrecv.at[:, pl.ds(1, ny - 1)], yr)
     state = [jnp.zeros((16, 128), F32)] * 2
     fall = jnp.ones((2, 128), F32)
     for s in range(ny):
@@ -315,26 +313,26 @@
     def x_row_copy(k):
         there = lax.rem(x + k, nx)
         return pltpu.make_async_remote_copy(
-            src_ref=xsend, dst_ref=xrecv.at[k], send_sem=xs.at[k], recv_sem=xr.at[k],
+            src_ref=xsend, dst_ref=xrecv.at[k], send_sem=xs, recv_sem=xr,
             device_id={"ctx_0": there}, device_id_type=MESH,
         )
 
     def x_fall_copy(k):
         there = lax.rem(x + k, nx)
         return pltpu.make_async_remote_copy(
-            src_ref=xfall, dst_ref=xfell.at[k], send_sem=es.at[k], recv_sem=er.at[k],
+            src_ref=xfall, dst_ref=xfell.at[k], send_sem=es, recv_sem=er,
             device_id={"ctx_0": there}, device_id_type=MESH,
         )
 
     def total_copy():
         return pltpu.make_async_remote_copy(
-            src_ref=xsend, dst_ref=row_in.at[x, place], send_sem=fs.at[0], recv_sem=fr.at[0, 4 * x + place],
+            src_ref=xsend, dst_ref=row_in.at[x, place], send_sem=fs.at[0], recv_sem=fr.at[0],
             device_id={"ctx_0": hub_x, "ctx_1": hub_y}, device_id_type=MESH,
         )
 
     def total_fall_copy():
         return pltpu.make_async_remote_copy(
-            src_ref=xfall, dst_ref=row_fell.at[x, place], send_sem=fs.at[1], recv_sem=fr.at[1, 4 * x + place],
+            src_ref=xfall, dst_ref=row_fell.at[x, place], send_sem=fs.at[1], recv_sem=fr.at[1],
             device_id={"ctx_0": hub_x, "ctx_1": hub_y}, device_id_type=MESH,
         )
 
@@ -345,8 +343,8 @@
 
     @pl.when(at_hub)
     def _():
-        pltpu.make_async_copy(xsend, row_in.at[x, place], fr.at[0, 4 * x + place]).start()
-        pltpu.make_async_copy(xfall, row_fell.at[x, place], fr.at[1, 4 * x + place]).start()
+        pltpu.make_async_copy(xsend, row_in.at[x, place], fr.at[0]).start()
+        pltpu.make_async_copy(xfall, row_fell.at[x, place], fr.at[1]).start()
 
     for k in far_first(nx):
         x_row_copy(k).start()
@@ -354,11 +352,9 @@
     xrecv[0] = xsend[...]
     xfell[0] = xfall[...]
 
-    lax.fori_loop(FIRST_PART, SECOND_PART, b_pass, 0)
-
-    for k in range(1, nx):
-        x_fall_copy(k).wait_recv()
-        x_row_copy(k).wait_recv()
+    if nx > 1:
+        wait_for(xfell.at[pl.ds(1, nx - 1)], er)
+        wait_for(xrecv.at[pl.ds(1, nx - 1)], xr)
     state = jnp.zeros((32, 128), F32)
     mine = state
     for s in range(nx):
@@ -370,7 +366,7 @@
     def back_copy(k):
         there = lax.rem(y + k, ny)
         return pltpu.make_async_remote_copy(
-            src_ref=back.at[there], dst_ref=before.at[k], send_sem=bs.at[k], recv_sem=br.at[k],
+            src_ref=back.at[there], dst_ref=before.at[k], send_sem=bs, recv_sem=br,
             device_id={"ctx_1": there}, device_id_type=MESH,
         )
 
@@ -380,11 +376,9 @@
         back_copy(k).start()
     before[0] = back[y]
 
-    lax.fori_loop(SECOND_PART, 8, b_pass, 0)
-
     def start_copy(to):
         return pltpu.make_async_remote_copy(
-            src_ref=staged.at[to], dst_ref=start, send_sem=gs.at[to], recv_sem=gr,
+            src_ref=staged.at[to], dst_ref=start, send_sem=gs, recv_sem=gr,
             device_id={"pair": to}, device_id_type=MESH,
         )
 
@@ -394,19 +388,19 @@
 
     @pl.when(is_hub)
     def _():
+        wait_for(row_fell, fr.at[1])
+        wait_for(row_in, fr.at[0])
+        wait_for(prompts.at[pl.ds(0, nz - 1)], tr)
         states = []
         for i in range(4):
             state = jnp.zeros((32, 128), F32)
             for s in range(nx):
-                pltpu.make_async_copy(xsend, row_in.at[s, i], fr.at[0, 4 * s + i]).wait()
-                pltpu.make_async_copy(xfall, row_fell.at[s, i], fr.at[1, 4 * s + i]).wait()
                 state = rows16(row_fell[s, i]) * state + row_in[s, i]
             states.append(state)
         for to in range(nz):
 
             @pl.when(p != to)
             def _(to=to):
-                tile_copy(to).wait_recv()
                 for i, state in enumerate(chosen(prompts[to], states)):
                     staged[to, 16 * i : 16 * i + 16, :] = state
                 start_copy(to).start()
@@ -439,8 +433,7 @@
             b_inner[second, :, lanes] = jnp.where(live, b_inner[second, :, lanes] + own * carried[:, lanes], 0.0)
             b_lead[second, :, lanes] = jnp.where(live, own * fall, 0.0)
 
-    for k in range(1, ny):
-        back_copy(k).wait_recv()
+    wait_for(before.at[pl.ds(1, ny - 1)], br)
     for j in range(8):
         slot = lax.rem(y - holder(j) + ny, ny)
         for pr in range(2):
@@ -451,14 +444,12 @@
         carried = dot(c_cols[u // 2], state_parts[u])
         prompt_outs[u] = (p_inner[u] + p_lead[u] * carried).astype(BF16)
 
-    for k in range(1, ny):
-        for pr in range(2):
-            y_copy(pr, k).wait_send()
-        fall_copy(k).wait_send()
-        back_copy(k).wait_send()
-    for k in range(1, nx):
-        x_row_copy(k).wait_send()
-        x_fall_copy(k).wait_send()
+    wait_for(ysend.at[:, pl.ds(0, ny - 1)], ys)
+    wait_for(yfall.at[pl.ds(0, ny - 1)], ds)
+    wait_for(back.at[pl.ds(0, ny - 1)], bs)
+    if nx > 1:
+        wait_for(xrecv.at[pl.ds(0, nx - 1)], xs)
+        wait_for(xfell.at[pl.ds(0, nx - 1)], es)
 
     @pl.when(from_hub)
     def _():
@@ -475,11 +466,7 @@
 
     @pl.when(is_hub)
     def _():
-        for to in range(nz):
-
-            @pl.when(p != to)
-            def _(to=to):
-                start_copy(to).wait_send()
+        wait_for(staged.at[pl.ds(0, nz - 1)], gs)
 
 
 def write_kernel(prompt_outs, b_inner, b_lead, start_parts, b_cols, py, by, outs, sem):
@@ -551,15 +538,15 @@
             pltpu.VMEM((nz, 8, 128), F32),
             pltpu.VMEM((nz, 64, 128), F32),
             pltpu.VMEM((64, 128), F32),
-            dma((13,)),
-            dma((2 * ny,)), dma((2 * ny,)),
-            dma((ny,)), dma((ny,)),
-            dma((nx,)), dma((nx,)),
-            dma((nx,)), dma((nx,)),
-            dma((ny,)), dma((ny,)),
-            dma((2,)), dma((2, 4 * nx)),
-            dma, dma((nz,)),
-            dma((nz,)), dma,
+            dma((8,)),
+            dma, dma,
+            dma, dma,
+            dma, dma,
+            dma, dma,
+            dma, dma,
+            dma((2,)), dma((2,)),
+            dma, dma,
+            dma, dma,
         ],
         compiler_params=pltpu.CompilerParams(
             collective_id=0, has_side_effects=True, vmem_limit_bytes=40 * 1024 * 1024

time: 33.3 us -> 32.1 us (0.964)
  Pallas kernels: 31.9 us -> 30.6 us
    pallas_call x1, Pallas kernels: 30.5 us -> 29.3 us  [body(): pl.pallas_call(functools.partial(kernel, nx, ny, nz), out_shape=between,...]
where the time goes in v3:
time: 32.1 us; the launch traced here: 31.9 us
  Pallas kernels  30.6 us (95%)
  between operations  1.29 us (4%)
    pallas_call x1, Pallas kernels, body(): pl.pallas_call(functools.partial(kernel, nx, ny, nz), out_shape=between,...  29.3 us
    pallas_call x1, Pallas kernels, body(): pl.pallas_call(write_kernel, out_shape=(jax.ShapeDtypeStruct(px.shape, BF...  1.39 us

profile of v3, /device:TPU:7, one launch (start us, length us, event | category | flops | bytes accessed | tf_op | source)
XLA Modules:
  0.0 31.9 jit_solution(11244978802071577885)
XLA Ops:
  1.3 29.3 %layer.1 = (bf16[4,256,512]{2,1,0:T(8,128)(2,1)S(1)}, f32[4,256,512]{2,1,0:T(8,128)S(1)}, f32[4,256,512]{2,1,0:T(8,128)S(1)}, bf16[128,512]{1,0:T(8,128)(2,1)S(1)}, bf16[4,256,128]{2,1,0:T(8,128)(2,1)S(1)}) custom-call(bf16[2,256,1024]{2,1,0:T(8,128)(2,1)} %px.1, bf16[2,2,16,256]{3,2,1,0:T(8,128)(2,1)} %pbc_in.1, f32[2,16,256]{2,1,0:T(8,128)} %pld_in.1, ...), custom_call_target="tpu_custom_call" | custom-call | tf_op jit(solution)/shard_map/layer/pallas_call | solution.py:501
  30.5 1.4 %write.1 = (bf16[2,256,1024]{2,1,0:T(8,128)(2,1)}, bf16[2,512,512]{2,1,0:T(8,128)(2,1)}) custom-call(bf16[4,256,512]{2,1,0:T(8,128)(2,1)S(1)} %get-tuple-element.7.prompt_outs, f32[4,256,512]{2,1,0:T(8,128)S(1)} %get-tuple-element.8.b_inner, f32[4,256,512]{2,1,0:T(8,128)S(1)} %get-tuple-element.9.b_lead, bf16[128,512]{1,0:T(8,128)(2,1)S(1)} %get-tuple-element.10.start_parts, ...), custom_call_target="tpu_custom_call" | custom-call | tf_op jit(solution)/shard_map/write/pallas_call | solution.py:556

commit v4 on v3

--- a/solution.py
+++ b/solution.py
@@ -470,21 +470,24 @@
 
 
 def write_kernel(prompt_outs, b_inner, b_lead, start_parts, b_cols, py, by, outs, sem):
-    copies = [
-        pltpu.make_async_copy(prompt_outs.at[u], py.at[u // 2, :, pl.ds(512 * (u % 2), 512)], sem.at[u])
-        for u in range(4)
-    ]
-    for copy in copies:
-        copy.start()
     for u in range(4):
-        outs[u] = (b_inner[u] + b_lead[u] * dot(b_cols[u], start_parts[...])).astype(BF16)
-        copy = pltpu.make_async_copy(
-            outs.at[u], by.at[u // 2, pl.ds(BLOCK * (u % 2), BLOCK), :], sem.at[4 + u]
-        )
-        copy.start()
-        copies.append(copy)
-    for copy in copies:
-        copy.wait()
+        pltpu.make_async_copy(
+            prompt_outs.at[u], py.at[u // 2, :, pl.ds(512 * (u % 2), 512)], sem.at[0]
+        ).start()
+    for u in range(4):
+        for row in range(0, BLOCK, 128):
+            rows = slice(row, row + 128)
+            for lane in range(0, 512, 256):
+                lanes = slice(lane, lane + 256)
+                carried = dot(b_cols[u, rows, :], start_parts[:, lanes])
+                outs[u, rows, lanes] = (b_inner[u, rows, lanes] + b_lead[u, rows, lanes] * carried).astype(BF16)
+            pltpu.make_async_copy(
+                outs.at[u, pl.ds(row, 128), :],
+                by.at[u // 2, pl.ds(BLOCK * (u % 2) + row, 128), :],
+                sem.at[1],
+            ).start()
+    wait_for(prompt_outs, sem.at[0])
+    wait_for(outs, sem.at[1])
 
 
 def body(nx, ny, nz, px, pbc, pld, bx, bbc, bld, bprompt, blen):
@@ -558,7 +561,7 @@
         out_shape=(jax.ShapeDtypeStruct(px.shape, BF16), jax.ShapeDtypeStruct(bx.shape, BF16)),
         in_specs=[vmem] * 5,
         out_specs=(any_space, any_space),
-        scratch_shapes=[pltpu.VMEM((4, BLOCK, 512), BF16), dma((8,))],
+        scratch_shapes=[pltpu.VMEM((4, BLOCK, 512), BF16), dma((2,))],
         compiler_params=pltpu.CompilerParams(vmem_limit_bytes=16 * 1024 * 1024),
         name="write",
     )(*kept)

time: 32.1 us -> 32 us (level)
  no operation moved by 1% of the time
where the time goes in v4:
time: 32 us; the launch traced here: 31.9 us
  Pallas kernels  30.6 us (96%)
  between operations  1.29 us (4%)
    pallas_call x1, Pallas kernels, body(): pl.pallas_call(functools.partial(kernel, nx, ny, nz), out_shape=between,...  29.3 us
    pallas_call x1, Pallas kernels, body(): pl.pallas_call(write_kernel, out_shape=(jax.ShapeDtypeStruct(px.shape, BF...  1.33 us

profile of v4, /device:TPU:7, one launch (start us, length us, event | category | flops | bytes accessed | tf_op | source)
XLA Modules:
  0.0 31.9 jit_solution(12646287231708989398)
XLA Ops:
  1.3 29.3 %layer.1 = (bf16[4,256,512]{2,1,0:T(8,128)(2,1)S(1)}, f32[4,256,512]{2,1,0:T(8,128)S(1)}, f32[4,256,512]{2,1,0:T(8,128)S(1)}, bf16[128,512]{1,0:T(8,128)(2,1)S(1)}, bf16[4,256,128]{2,1,0:T(8,128)(2,1)S(1)}) custom-call(bf16[2,256,1024]{2,1,0:T(8,128)(2,1)} %px.1, bf16[2,2,16,256]{3,2,1,0:T(8,128)(2,1)} %pbc_in.1, f32[2,16,256]{2,1,0:T(8,128)} %pld_in.1, ...), custom_call_target="tpu_custom_call" | custom-call | tf_op jit(solution)/shard_map/layer/pallas_call | solution.py:504
  30.5 1.3 %write.1 = (bf16[2,256,1024]{2,1,0:T(8,128)(2,1)}, bf16[2,512,512]{2,1,0:T(8,128)(2,1)}) custom-call(bf16[4,256,512]{2,1,0:T(8,128)(2,1)S(1)} %get-tuple-element.7.prompt_outs, f32[4,256,512]{2,1,0:T(8,128)S(1)} %get-tuple-element.8.b_inner, f32[4,256,512]{2,1,0:T(8,128)S(1)} %get-tuple-element.9.b_lead, bf16[128,512]{1,0:T(8,128)(2,1)S(1)} %get-tuple-element.10.start_parts, ...), custom_call_target="tpu_custom_call" | custom-call | tf_op jit(solution)/shard_map/write/pallas_call | solution.py:559
